TPU v7x, 32 devices: a whole 2x2x4 slice. The times are simulated.
32 devices in a mesh: group: 1, image: 4 (over z), prow: 4 (over y, x), pcol: 2 (over core).
Axes of the slice: x: 2, y: 2, z: 4, core: 2. Of those that a mesh axis runs over, the one named last changes fastest.
Arguments:
- latent: bfloat16 [4, 32, 64, 640], P(('group', 'image'), 'prow', 'pcol'), may hold values from -6 to 6
- conv_weight: bfloat16 [3, 3, 640, 640], replicated, may hold values from -0.078125 to 0.078125
- w_query: bfloat16 [640, 640], replicated, may hold values from -2 to 2
- w_key: bfloat16 [640, 640], replicated, may hold values from -2 to 2
- w_value: bfloat16 [640, 640], replicated, may hold values from -0.25 to 0.25
- w_out: bfloat16 [640, 640], replicated, may hold values from -0.25 to 0.25
- anchor_index: int32 [4], P('group'), may hold values from 0 to 3, as said below
- block_order: int32 [4, 16], P('group'), may hold values from 0 to 15, each once within a row
- block_count: int32 [4], P('group'), may hold values from 1 to 4, as said below
Outputs:
- features: bfloat16 [4, 32, 64, 640], P(('group', 'image'), 'prow', 'pcol')
- attended: bfloat16 [4, 32, 64, 640], P(('group', 'image'), 'prow', 'pcol')
Inputs may be any that keep to these rules, and one draw needn't show every extreme that they name: `anchor_index`: 4 different images of the batch. `block_count`: some anchor has 4 subject blocks.
All inputs are finite; a program needn't handle non-finite values.
Results may differ from a plain program's by a relative error of at most 0.017.
Values may be sent and summed in bfloat16 or wider, within the bound.
No kernel may reach another device: no remote copies, remote signals or barrier semaphores. Data moves between devices by JAX's collectives and lax.ppermute only.
A program may use at most 128 MiB of HBM per device.

v0:
```python
import jax
import jax.numpy as jnp
from jax import lax
from jax.sharding import PartitionSpec as P

HEAD_DIM = 64
BLOCK = 128
ANCHORS = 4
NSEL = 4


def extended(cells, sides, width):
    for axis, dim in sides:
        count = lax.axis_size(axis)
        ends = count - 1
        head = lax.slice_in_dim(cells, 0, width, axis=dim)
        tail = lax.slice_in_dim(cells, cells.shape[dim] - width, cells.shape[dim], axis=dim)
        cells = jnp.concatenate(
            [
                lax.ppermute(tail, axis, [(i, (i + 1) % count) for i in range(ends)]),
                cells,
                lax.ppermute(head, axis, [((i + 1) % count, i) for i in range(ends)]),
            ],
            axis=dim,
        )
    return cells


def from_root(block, axis, holder):
    block = jnp.where(lax.axis_index(axis) == holder, block, jnp.zeros_like(block))
    return lax.psum(block, axis)


def layer_norm(values):
    centered = values - jnp.mean(values, axis=-1, keepdims=True)
    spread = jnp.mean(centered * centered, axis=-1, keepdims=True)
    return centered * lax.rsqrt(spread + 1e-05)


def grouped_attention(query_cols, every_kv, allowed, group_heads):
    span_cols = group_heads * HEAD_DIM
    value_start = every_kv.shape[1] // 2

    def one_group(group_number):
        offset_col = group_number * span_cols
        group_query = lax.dynamic_slice_in_dim(query_cols, offset_col, span_cols, 1).reshape(
            -1, group_heads, HEAD_DIM
        )
        group_key = lax.dynamic_slice_in_dim(every_kv, offset_col, span_cols, 1).reshape(
            -1, group_heads, HEAD_DIM
        )
        group_value = lax.dynamic_slice_in_dim(
            every_kv, value_start + offset_col, span_cols, 1
        ).reshape(-1, group_heads, HEAD_DIM)
        scores = jnp.einsum(
            "qhd,khd->hqk", group_query, group_key, preferred_element_type=jnp.float32
        ) * HEAD_DIM ** (-0.5)
        scores = jnp.where(allowed[None, None, :], scores, -jnp.inf)
        peak = jnp.max(scores, axis=2, keepdims=True)
        exponent = jnp.exp(scores - peak)
        probs = (exponent / jnp.sum(exponent, axis=2, keepdims=True)).astype(jnp.bfloat16)
        group_out = jnp.einsum(
            "hqk,khd->qhd", probs, group_value, preferred_element_type=jnp.float32
        ).astype(jnp.bfloat16)
        return group_out.reshape(-1, span_cols)

    head_outs = lax.map(one_group, jnp.arange(query_cols.shape[1] // span_cols))
    return head_outs.transpose(1, 0, 2).reshape(-1, query_cols.shape[1])


def shards(
    latent, conv_weight, w_query, w_key, w_value, w_out, anchor_index, block_order, block_count
):
    tile_rows, tile_cols, channels = (latent.shape[1], latent.shape[2], latent.shape[3])
    activated = jax.nn.silu(latent.astype(jnp.float32)).astype(jnp.bfloat16)
    padded = extended(activated, (("prow", 1), ("pcol", 2)), 1)
    running = latent.astype(jnp.float32)
    for row_tap in range(3):
        for col_tap in range(3):
            window = padded[:, row_tap : row_tap + tile_rows, col_tap : col_tap + tile_cols, :]
            running = running + jnp.dot(
                window, conv_weight[row_tap, col_tap], preferred_element_type=jnp.float32
            )
    features = running.astype(jnp.bfloat16)
    tokens = features.reshape(-1, channels)
    normed = layer_norm(tokens.astype(jnp.float32)).astype(jnp.bfloat16)
    queries = jnp.dot(normed, w_query, preferred_element_type=jnp.float32).astype(jnp.bfloat16)
    key_part = jnp.dot(normed, w_key, preferred_element_type=jnp.float32).astype(jnp.bfloat16)
    value_part = jnp.dot(normed, w_value, preferred_element_type=jnp.float32).astype(jnp.bfloat16)
    live_slots = jnp.arange(NSEL)[None, :] < block_count[:, None]
    anchor_live = jnp.repeat(live_slots.reshape(-1), BLOCK)
    keyvals = jnp.concatenate([key_part, value_part], axis=1)
    image_kv = lax.all_gather(keyvals, ("prow", "pcol"), axis=0, tiled=True)
    blocks = image_kv.reshape(-1, BLOCK, 2 * channels)
    patch_count = lax.axis_size("prow") * lax.axis_size("pcol")
    share_rows = NSEL * BLOCK // patch_count
    position = lax.axis_index("prow") * lax.axis_size("pcol") + lax.axis_index("pcol")
    received = []
    for anchor in range(ANCHORS):
        picked = blocks[block_order[anchor, :NSEL]].reshape(NSEL * BLOCK, 2 * channels)
        portion = lax.dynamic_slice_in_dim(picked, position * share_rows, share_rows, 0)
        received.append(from_root(portion, "image", anchor_index[anchor]))
    joined = lax.all_gather(jnp.stack(received, axis=0), ("prow", "pcol"), axis=1, tiled=True)
    anchor_kv = joined.reshape(ANCHORS * NSEL * BLOCK, 2 * channels)
    allowed = jnp.concatenate([jnp.ones((image_kv.shape[0],), jnp.bool_), anchor_live])
    every_kv = jnp.concatenate([image_kv, anchor_kv], axis=0)
    merged = grouped_attention(queries, every_kv, allowed, 2)
    attended = jnp.dot(merged, w_out, preferred_element_type=jnp.float32).astype(jnp.bfloat16)
    return (features, attended.reshape(latent.shape))


def solution(mesh):
    placed = (
        P(("group", "image"), "prow", "pcol", None),
        P(),
        P(),
        P(),
        P(),
        P(),
        P("group"),
        P("group", None),
        P("group"),
    )
    return jax.shard_map(
        shards,
        mesh=mesh,
        in_specs=placed,
        out_specs=(
            P(("group", "image"), "prow", "pcol", None),
            P(("group", "image"), "prow", "pcol", None),
        ),
        check_vma=False,
    )
```

profile of v0, /device:TPU:0, one launch (start us, length us, event | category | flops | bytes accessed | tf_op | source)
XLA Modules:
  0.0 259.8 jit_solution(5241671841525524650)
XLA Ops:
  8.6 5.1 %collective-permute-start = (bf16[1,1,32,640]{3,2,1,0:T(8,128)(2,1)S(1)}, bf16[1,1,32,640]{3,2,1,0:T(8,128)(2,1)S(1)}, u32[]{:S(2)}, u32[]{:S(2)}) collective-permute-start(bf16[1,1,32,640]{3,2,1,0:T(8,128)(2,1)S(1)} %get-tuple-element.108), channel_id=1, source_target_pairs={{0,2},{2,4},{4,6},{1,3},{3,5},{5,7},{8,10},{10,12},{12,14},{9,11},... | collective-permute-start | bytes 122888 | tf_op jit(solution)/shard_map/ppermute | solution.py:20
  16.8 2.8 %collective-permute-done.1 = bf16[1,1,32,640]{3,2,1,0:T(8,128)(2,1)S(1)} collective-permute-done((bf16[1,1,32,640]{3,2,1,0:T(8,128)(2,1)S(1)}, bf16[1,1,32,640]{3,2,1,0:T(8,128)(2,1)S(1)}, u32[]{:S(2)}, u32[]{:S(2)}) %collective-permute-start.1) | collective-permute-done | bytes 40992 | tf_op jit(solution)/shard_map/ppermute | solution.py:22
  33.4 40.0 %all-gather.3.cloned.1.call-done = bf16[2048,1280]{1,0:T(8,128)(2,1)} async-done(((bf16[256,1280]{1,0:T(8,128)(2,1)}), bf16[2048,1280]{1,0:T(8,128)(2,1)}) %all-gather.3.cloned.1.call-update) | async-done | bytes 5242896 | tf_op jit(solution)/shard_map/all_gather | solution.py:93
  73.4 4.3 %gather_fusion.2 = bf16[4,128,1280]{2,1,0:T(8,128)(2,1)} fusion(bf16[16,128,1280]{2,1,0:T(8,128)(2,1)} %bitcast.203, s32[1024]{0:T(1024)S(1)} %get-tuple-element.121), kind=kCustom, calls=%fused_computation.2 | custom fusion | bytes 2621456 | tf_op jit(solution)/shard_map/gather | solution.py:100
  77.6 4.2 %gather_fusion.1 = bf16[4,128,1280]{2,1,0:T(8,128)(2,1)} fusion(bf16[16,128,1280]{2,1,0:T(8,128)(2,1)} %bitcast.204, s32[1024]{0:T(1024)S(1)} %get-tuple-element.122), kind=kCustom, calls=%fused_computation.1 | custom fusion | bytes 2621456 | tf_op jit(solution)/shard_map/gather | solution.py:100
  81.8 4.2 %gather_fusion = bf16[4,128,1280]{2,1,0:T(8,128)(2,1)} fusion(bf16[16,128,1280]{2,1,0:T(8,128)(2,1)} %bitcast.205, s32[1024]{0:T(1024)S(1)} %get-tuple-element.123), kind=kCustom, calls=%fused_computation | custom fusion | bytes 2621456 | tf_op jit(solution)/shard_map/gather | solution.py:100
  86.0 3.1 %gather_fusion.3 = bf16[4,128,1280]{2,1,0:T(8,128)(2,1)S(1)} fusion(bf16[16,128,1280]{2,1,0:T(8,128)(2,1)} %bitcast.206, s32[1024]{0:T(1024)S(1)} %get-tuple-element.120), kind=kCustom, calls=%fused_computation.3 | custom fusion | bytes 2621456 | tf_op jit(solution)/shard_map/gather | solution.py:100
  94.8 40.7 %all-reduce.4.cloned.1.call-done = (bf16[1,64,1280]{2,1,0:T(8,128)(2,1)}, bf16[1,64,1280]{2,1,0:T(8,128)(2,1)}, bf16[1,64,1280]{2,1,0:T(8,128)(2,1)}, bf16[1,64,1280]{2,1,0:T(8,128)(2,1)}) async-done(((bf16[1,64,1280]{2,1,0:T(8,128)(2,1)}, bf16[1,64,1280]{2,1,0:T(8,128)(2,1)}, bf16[1,64,1280]{2,1,0:T(8,128)(2,1)}, bf16[1,64,1280]{2,1,0:T(8,128)(2,1)}), (bf16[1,64,1280]{2,1,0:T(8,128)(2,1)}, ...) | async-done | bytes 655376 | tf_op jit(solution)/shard_map/psum | solution.py:31
  135.5 2.1 pad_maximum_fusion.2
  139.4 39.0 %all-gather.5.cloned.1.call-done = bf16[4,512,1280]{2,1,0:T(8,128)(2,1)} async-done(((bf16[4,64,1280]{2,1,0:T(8,128)(2,1)}), bf16[4,512,1280]{2,1,0:T(8,128)(2,1)}) %all-gather.5.cloned.1.call-update) | async-done | bytes 5242896 | tf_op jit(solution)/shard_map/all_gather | solution.py:103
  178.4 9.9 %pad_maximum_fusion = bf16[4096,1280]{1,0:T(8,128)(2,1)} fusion(bf16[2048,1280]{1,0:T(8,128)(2,1)} %bitcast.207, bf16[2048,1280]{1,0:T(8,128)(2,1)} %all-gather.3.cloned.1.call-done), kind=kLoop, calls=%fused_computation.23 | loop fusion | flops 20971520 | bytes 20971520 | tf_op jit(solution)/shard_map/concatenate | solution.py:106
  188.3 14.3 %copy.11 = bf16[4096,1280]{0,1:T(8,128)(2,1)} copy(bf16[4096,1280]{1,0:T(8,128)(2,1)} %pad_maximum_fusion) | data formatting | bytes 20971520 | tf_op jit(solution)/shard_map/while | solution.py:67
  202.6 48.2 %while.12 = (s32[]{:T(128)}, bf16[5,256,128]{1,2,0:T(8,128)(2,1)}, s32[5]{0:T(128)S(1)}, bf16[4096,1280]{0,1:T(8,128)(2,1)}, pred[4096]{0:T(1024)(128)(4,1)S(1)}...) while((s32[]{:T(128)}, bf16[5,256,128]{1,2,0:T(8,128)(2,1)}, ...), condition=%wide.region_9.10_spmd, body=%wide.region_6.9_spmd.sunk | while | flops 824222208 | bytes 7942902 | solution.py:67
  205.7 3.0 %fusion.91 = f32[2,256]{1,0:T(2,128)S(1)} fusion(pred[4096]{0:T(1024)(128)(4,1)S(1)} %get-tuple-element.193, bf16[256,2,64]{0,2,1:T(8,128)(2,1)S(1)} %bitcast.212, bf16[4096,2,64]{0,2,1:T(8,128)(2,1)S(1)} %bitcast.200), kind=kOutput, calls=%fused_computation.118.clone.1 | convolution fusion | flops 276828160 | bytes 1120256 | tf_op jit(solution)/shard_map/while/body/eval_jaxpr/sub | solution.py:60
  208.7 2.9 %fusion.92 = bf16[2,64,256]{2,1,0:T(8,128)(2,1)S(1)} fusion(bf16[4096,2,64]{0,2,1:T(8,128)(2,1)S(1)} %bitcast.202, f32[2,256]{1,0:T(2,128)S(1)} %fusion.91, pred[4096]{0:T(1024)(128)(4,1)S(1)} %get-tuple-element.193, bf16[256,2,64]{0,2,1:T(8,128)(2,1)S(1)} %bitcast.213, bf16[4096,2,64]{0,2,1:T(8,128)(2,1)S(1)} %bitcast.201), kind=kOutput, calls=%fused_computation.14.clone.1 | convolution fusion | flops 547394048 | bytes 2234368 | tf_op jit(solution)/shard_map/while/body/eval_jaxpr/hqk,khd->qhd/dot_general | solution.py:62
  215.3 3.0 %fusion.91 = f32[2,256]{1,0:T(2,128)S(1)} fusion(pred[4096]{0:T(1024)(128)(4,1)S(1)} %get-tuple-element.193, bf16[256,2,64]{0,2,1:T(8,128)(2,1)S(1)} %bitcast.212, bf16[4096,2,64]{0,2,1:T(8,128)(2,1)S(1)} %bitcast.200), kind=kOutput, calls=%fused_computation.118.clone.1 | convolution fusion | flops 276828160 | bytes 1120256 | tf_op jit(solution)/shard_map/while/body/eval_jaxpr/sub | solution.py:60
  218.3 2.9 %fusion.92 = bf16[2,64,256]{2,1,0:T(8,128)(2,1)S(1)} fusion(bf16[4096,2,64]{0,2,1:T(8,128)(2,1)S(1)} %bitcast.202, f32[2,256]{1,0:T(2,128)S(1)} %fusion.91, pred[4096]{0:T(1024)(128)(4,1)S(1)} %get-tuple-element.193, bf16[256,2,64]{0,2,1:T(8,128)(2,1)S(1)} %bitcast.213, bf16[4096,2,64]{0,2,1:T(8,128)(2,1)S(1)} %bitcast.201), kind=kOutput, calls=%fused_computation.14.clone.1 | convolution fusion | flops 547394048 | bytes 2234368 | tf_op jit(solution)/shard_map/while/body/eval_jaxpr/hqk,khd->qhd/dot_general | solution.py:62
  225.0 3.0 %fusion.91 = f32[2,256]{1,0:T(2,128)S(1)} fusion(pred[4096]{0:T(1024)(128)(4,1)S(1)} %get-tuple-element.193, bf16[256,2,64]{0,2,1:T(8,128)(2,1)S(1)} %bitcast.212, bf16[4096,2,64]{0,2,1:T(8,128)(2,1)S(1)} %bitcast.200), kind=kOutput, calls=%fused_computation.118.clone.1 | convolution fusion | flops 276828160 | bytes 1120256 | tf_op jit(solution)/shard_map/while/body/eval_jaxpr/sub | solution.py:60
  228.0 2.9 %fusion.92 = bf16[2,64,256]{2,1,0:T(8,128)(2,1)S(1)} fusion(bf16[4096,2,64]{0,2,1:T(8,128)(2,1)S(1)} %bitcast.202, f32[2,256]{1,0:T(2,128)S(1)} %fusion.91, pred[4096]{0:T(1024)(128)(4,1)S(1)} %get-tuple-element.193, bf16[256,2,64]{0,2,1:T(8,128)(2,1)S(1)} %bitcast.213, bf16[4096,2,64]{0,2,1:T(8,128)(2,1)S(1)} %bitcast.201), kind=kOutput, calls=%fused_computation.14.clone.1 | convolution fusion | flops 547394048 | bytes 2234368 | tf_op jit(solution)/shard_map/while/body/eval_jaxpr/hqk,khd->qhd/dot_general | solution.py:62
  234.6 3.0 %fusion.91 = f32[2,256]{1,0:T(2,128)S(1)} fusion(pred[4096]{0:T(1024)(128)(4,1)S(1)} %get-tuple-element.193, bf16[256,2,64]{0,2,1:T(8,128)(2,1)S(1)} %bitcast.212, bf16[4096,2,64]{0,2,1:T(8,128)(2,1)S(1)} %bitcast.200), kind=kOutput, calls=%fused_computation.118.clone.1 | convolution fusion | flops 276828160 | bytes 1120256 | tf_op jit(solution)/shard_map/while/body/eval_jaxpr/sub | solution.py:60
  237.6 2.9 %fusion.92 = bf16[2,64,256]{2,1,0:T(8,128)(2,1)S(1)} fusion(bf16[4096,2,64]{0,2,1:T(8,128)(2,1)S(1)} %bitcast.202, f32[2,256]{1,0:T(2,128)S(1)} %fusion.91, pred[4096]{0:T(1024)(128)(4,1)S(1)} %get-tuple-element.193, bf16[256,2,64]{0,2,1:T(8,128)(2,1)S(1)} %bitcast.213, bf16[4096,2,64]{0,2,1:T(8,128)(2,1)S(1)} %bitcast.201), kind=kOutput, calls=%fused_computation.14.clone.1 | convolution fusion | flops 547394048 | bytes 2234368 | tf_op jit(solution)/shard_map/while/body/eval_jaxpr/hqk,khd->qhd/dot_general | solution.py:62
  244.2 3.0 %fusion.91 = f32[2,256]{1,0:T(2,128)S(1)} fusion(pred[4096]{0:T(1024)(128)(4,1)S(1)} %get-tuple-element.193, bf16[256,2,64]{0,2,1:T(8,128)(2,1)S(1)} %bitcast.212, bf16[4096,2,64]{0,2,1:T(8,128)(2,1)S(1)} %bitcast.200), kind=kOutput, calls=%fused_computation.118.clone.1 | convolution fusion | flops 276828160 | bytes 1120256 | tf_op jit(solution)/shard_map/while/body/eval_jaxpr/sub | solution.py:60
  247.3 2.9 %fusion.92 = bf16[2,64,256]{2,1,0:T(8,128)(2,1)S(1)} fusion(bf16[4096,2,64]{0,2,1:T(8,128)(2,1)S(1)} %bitcast.202, f32[2,256]{1,0:T(2,128)S(1)} %fusion.91, pred[4096]{0:T(1024)(128)(4,1)S(1)} %get-tuple-element.193, bf16[256,2,64]{0,2,1:T(8,128)(2,1)S(1)} %bitcast.213, bf16[4096,2,64]{0,2,1:T(8,128)(2,1)S(1)} %bitcast.201), kind=kOutput, calls=%fused_computation.14.clone.1 | convolution fusion | flops 547394048 | bytes 2234368 | tf_op jit(solution)/shard_map/while/body/eval_jaxpr/hqk,khd->qhd/dot_general | solution.py:62
  250.8 2.5 convolution_convert_fusion
  (90 shorter events, 38.2 us)
Async XLA Ops:
  7.2 21.2 %copy-start = (bf16[640,640]{1,0:T(8,128)(2,1)S(1)}, bf16[640,640]{1,0:T(8,128)(2,1)}, u32[]{:S(2)}) copy-start(bf16[640,640]{1,0:T(8,128)(2,1)} %param.15) | copy-start | bytes 2457604
  7.2 66.2 %all-gather.3.cloned.1.call-start = ((), (), s32[]{:S(2)}) async-start(), calls=%async_computation | async-start | bytes 5898240 | tf_op jit(solution)/shard_map/all_gather | solution.py:93
  7.2 16.8 %copy-start.3 = (bf16[3,3,640,640]{3,2,1,0:T(8,128)(2,1)S(1)}, bf16[3,3,640,640]{3,2,1,0:T(8,128)(2,1)}, u32[]{:S(2)}) copy-start(bf16[3,3,640,640]{3,2,1,0:T(8,128)(2,1)} %param.12) | copy-start | bytes 22118404
  8.6 8.2 %collective-permute-start = (bf16[1,1,32,640]{3,2,1,0:T(8,128)(2,1)S(1)}, bf16[1,1,32,640]{3,2,1,0:T(8,128)(2,1)S(1)}, u32[]{:S(2)}, u32[]{:S(2)}) collective-permute-start(bf16[1,1,32,640]{3,2,1,0:T(8,128)(2,1)S(1)} %get-tuple-element.108), channel_id=1, source_target_pairs={{0,2},{2,4},{4,6},{1,3},{3,5},{5,7},{8,10},{10,12},{12,14},{9,11},... | collective-permute-start | bytes 122888 | tf_op jit(solution)/shard_map/ppermute | solution.py:20
  13.7 5.9 %collective-permute-start.1 = (bf16[1,1,32,640]{3,2,1,0:T(8,128)(2,1)S(1)}, bf16[1,1,32,640]{3,2,1,0:T(8,128)(2,1)S(1)}, u32[]{:S(2)}, u32[]{:S(2)}) collective-permute-start(bf16[1,1,32,640]{3,2,1,0:T(8,128)(2,1)S(1)} %get-tuple-element.109), channel_id=1, source_target_pairs={{2,0},{4,2},{6,4},{3,1},{5,3},{7,5},{10,8},{12,10},{14,12},{11,9},... | collective-permute-start | bytes 122888 | tf_op jit(solution)/shard_map/ppermute | solution.py:22
  19.7 4.8 %collective-permute-start.2 = (bf16[1,10,1,640]{3,2,1,0:T(2,128)(2,1)S(1)}, bf16[1,10,1,640]{3,2,1,0:T(2,128)(2,1)S(1)}, u32[]{:S(2)}, u32[]{:S(2)}) collective-permute-start(bf16[1,10,1,640]{3,2,1,0:T(2,128)(2,1)S(1)} %get-tuple-element.106), channel_id=1, source_target_pairs={{0,1},{2,3},{4,5},{6,7},{8,9},{10,11},{12,13},{14,15},{16,17},{18,... | collective-permute-start | bytes 38408 | tf_op jit(solution)/shard_map/ppermute | solution.py:20
  21.0 6.1 %copy-start.2 = (bf16[1,8,32,640]{3,2,1,0:T(8,128)(2,1)S(1)}, bf16[1,8,32,640]{3,2,1,0:T(8,128)(2,1)}, u32[]{:S(2)}) copy-start(bf16[1,8,32,640]{3,2,1,0:T(8,128)(2,1)} %param.11) | copy-start | bytes 983044
  21.0 3.5 %collective-permute-start.3 = (bf16[1,10,1,640]{3,2,1,0:T(2,128)(2,1)S(1)}, bf16[1,10,1,640]{3,2,1,0:T(2,128)(2,1)S(1)}, u32[]{:S(2)}, u32[]{:S(2)}) collective-permute-start(bf16[1,10,1,640]{3,2,1,0:T(2,128)(2,1)S(1)} %get-tuple-element.107), channel_id=1, source_target_pairs={{1,0},{3,2},{5,4},{7,6},{9,8},{11,10},{13,12},{15,14},{17,16},{19,... | collective-permute-start | bytes 38408 | tf_op jit(solution)/shard_map/ppermute | solution.py:22
  25.6 3.2 %copy-start.4 = (bf16[640,640]{1,0:T(8,128)(2,1)S(1)}, bf16[640,640]{1,0:T(8,128)(2,1)}, u32[]{:S(2)}) copy-start(bf16[640,640]{1,0:T(8,128)(2,1)} %param.14) | copy-start | bytes 2457604
  26.6 3.7 %copy-start.5 = (s32[4]{0:T(128)S(1)}, s32[4]{0:T(128)}, u32[]{:S(2)}) copy-start(s32[4]{0:T(128)} %param.17) | copy-start | bytes 52
  26.6 6.7 %copy-start.6 = (s32[4,16]{1,0:T(4,128)S(1)}, s32[4,16]{1,0:T(4,128)}, u32[]{:S(2)}) copy-start(s32[4,16]{1,0:T(4,128)} %param.18) | copy-start | bytes 772
  27.8 61.4 %copy-start.1 = (bf16[1,8,32,640]{3,2,1,0:T(8,128)(2,1)}, bf16[1,8,32,640]{3,2,1,0:T(8,128)(2,1)S(1)}, u32[]{:S(2)}) copy-start(bf16[1,8,32,640]{3,2,1,0:T(8,128)(2,1)S(1)} %get-tuple-element.119) | copy-start | bytes 983044
  30.2 107.3 %copy-start.7 = (s32[4]{0:T(128)S(1)}, s32[4]{0:T(128)}, u32[]{:S(2)}) copy-start(s32[4]{0:T(128)} %param.19) | copy-start | bytes 52
  30.3 105.2 %all-reduce.4.cloned.1.call-start = ((), (), s32[]{:S(2)}) async-start(), calls=%async_computation.2 | async-start | bytes 1310720 | tf_op jit(solution)/shard_map/psum | solution.py:31
  94.7 83.7 %all-gather.5.cloned.1.call-start = ((), (), s32[]{:S(2)}) async-start(), calls=%async_computation.1 | async-start | bytes 5898240 | tf_op jit(solution)/shard_map/all_gather | solution.py:103
Sparse Core Ops, SparseCore 0:
  30.4 42.9 all-gather.2
  94.8 40.5 all-reduce.3
  137.7 40.7 all-gather.4
where the time goes:
time: 261 us; the launch traced here: 260 us
  waiting for transfers between devices  123 us (47%)
  local copies, waits for them, and re-layouts  46.3 us (18%)
  matrix products  41.2 us (16%)
  other arithmetic  20.5 us (8%)
  between operations  16.5 us (6%)
  starting transfers between devices  9.26 us (4%)
  loops' own time  3.44 us (1%)
    psum x1, waiting for transfers between devices, from_root(): return lax.psum(block, axis)  40.7 us
    all_gather x1, waiting for transfers between devices, shards(): image_kv = lax.all_gather(keyvals, ('prow', 'pcol'), axis=0, tiled=True)  40 us
    all_gather x1, waiting for transfers between devices, shards(): lax.all_gather(jnp.stack(received, axis=0), ('prow', 'pcol'), axis=1, til...  39 us
    gather x4, local copies, waits for them, and re-layouts, shards(): blocks[block_order[anchor, :NSEL]].reshape(NSEL * BLOCK, 2 * channels)  15.8 us
    sub x5, matrix products, one_group(): exponent = jnp.exp(scores - peak)  15.1 us
    dot_general x5, matrix products, one_group(): jnp.einsum('hqk,khd->qhd', probs, group_value, preferred_element_type=jnp...  14.4 us
    while x1, local copies, waits for them, and re-layouts, grouped_attention(): head_outs = lax.map(one_group, jnp.arange(query_cols.shape[1] // span_cols))  14.3 us
    concatenate x1, other arithmetic, shards(): every_kv = jnp.concatenate([image_kv, anchor_kv], axis=0)  9.91 us
  transfers between devices with their start and end apart: 7, of which 4 were waited for; matrix products, arithmetic and copies ran while one was open for 2% of the time, Pallas kernels for 0%

commit v1 on v0

--- a/solution.py
+++ b/solution.py
@@ -7,6 +7,12 @@
 BLOCK = 128
 ANCHORS = 4
 NSEL = 4
+
+
+def summed_here(value, name):
+    blocks = lax.all_gather(value, name, axis=0, tiled=False)
+    total = blocks.sum(axis=0)
+    return total
 
 
 def extended(cells, sides, width):
@@ -28,7 +34,7 @@
 
 def from_root(block, axis, holder):
     block = jnp.where(lax.axis_index(axis) == holder, block, jnp.zeros_like(block))
-    return lax.psum(block, axis)
+    return summed_here(block, axis)
 
 
 def layer_norm(values):

time: 261 us -> 280 us (1.073)
  blocking collectives: 0 us -> 66.5 us
  waiting for transfers between devices: 123 us -> 81.5 us
  other arithmetic: 20.5 us -> 15.2 us
    all_gather x0 -> x4, blocking collectives: none -> 66.5 us  [summed_here(): blocks = lax.all_gather(value, name, axis=0, tiled=False)]
    psum x1 -> x0, waiting for transfers between devices: 40.7 us -> none  [from_root(): return lax.psum(block, axis)]
    another operation x5 -> x1, other arithmetic: 7.6 us -> 0.94 us  [shards(): jnp.stack(received, axis=0)]
  transfers between devices with their start and end apart: 7 -> 6, of which waited for: 4 -> 3; matrix products, arithmetic and copies ran while one was open for 2% -> 2% of each run, Pallas kernels for 0% -> 0%
where the time goes in v1:
time: 280 us; the launch traced here: 278 us
  waiting for transfers between devices  81.5 us (29%)
  blocking collectives  66.5 us (24%)
  local copies, waits for them, and re-layouts  44.2 us (16%)
  matrix products  41.2 us (15%)
  between operations  17 us (6%)
  other arithmetic  15.2 us (5%)
  starting transfers between devices  9.22 us (3%)
  loops' own time  3.64 us (1%)
    all_gather x4, blocking collectives, summed_here(): blocks = lax.all_gather(value, name, axis=0, tiled=False)  66.5 us
    all_gather x1, waiting for transfers between devices, shards(): image_kv = lax.all_gather(keyvals, ('prow', 'pcol'), axis=0, tiled=True)  39.8 us
    all_gather x1, waiting for transfers between devices, shards(): lax.all_gather(jnp.stack(received, axis=0), ('prow', 'pcol'), axis=1, til...  38.8 us
    sub x5, matrix products, one_group(): exponent = jnp.exp(scores - peak)  15.1 us
    dot_general x5, matrix products, one_group(): jnp.einsum('hqk,khd->qhd', probs, group_value, preferred_element_type=jnp...  14.4 us
    while x1, local copies, waits for them, and re-layouts, grouped_attention(): head_outs = lax.map(one_group, jnp.arange(query_cols.shape[1] // span_cols))  14.3 us
    gather x4, local copies, waits for them, and re-layouts, shards(): blocks[block_order[anchor, :NSEL]].reshape(NSEL * BLOCK, 2 * channels)  13.6 us
    concatenate x1, other arithmetic, shards(): every_kv = jnp.concatenate([image_kv, anchor_kv], axis=0)  9.74 us
  transfers between devices with their start and end apart: 6, of which 3 were waited for; matrix products, arithmetic and copies ran while one was open for 2% of the time, Pallas kernels for 0%

profile of v1, /device:TPU:0, one launch (start us, length us, event | category | flops | bytes accessed | tf_op | source)
XLA Modules:
  0.0 278.5 jit_solution(10333131218956942485)
XLA Ops:
  8.6 5.1 %collective-permute-start = (bf16[1,1,32,640]{3,2,1,0:T(8,128)(2,1)S(1)}, bf16[1,1,32,640]{3,2,1,0:T(8,128)(2,1)S(1)}, u32[]{:S(2)}, u32[]{:S(2)}) collective-permute-start(bf16[1,1,32,640]{3,2,1,0:T(8,128)(2,1)S(1)} %get-tuple-element.104), channel_id=1, source_target_pairs={{0,2},{2,4},{4,6},{1,3},{3,5},{5,7},{8,10},{10,12},{12,14},{9,11},... | collective-permute-start | bytes 122888 | tf_op jit(solution)/shard_map/ppermute | solution.py:26
  33.6 39.8 %all-gather.7.cloned.1.call-done = bf16[2048,1280]{1,0:T(8,128)(2,1)} async-done(((bf16[256,1280]{1,0:T(8,128)(2,1)}), bf16[2048,1280]{1,0:T(8,128)(2,1)}) %all-gather.7.cloned.1.call-update) | async-done | bytes 5242896 | tf_op jit(solution)/shard_map/all_gather | solution.py:99
  73.3 3.1 %gather_fusion = bf16[4,128,1280]{2,1,0:T(8,128)(2,1)S(1)} fusion(bf16[16,128,1280]{2,1,0:T(8,128)(2,1)} %bitcast.203, s32[1024]{0:T(1024)S(1)} %get-tuple-element.119), kind=kCustom, calls=%fused_computation | custom fusion | bytes 2621456 | tf_op jit(solution)/shard_map/gather | solution.py:106
  76.5 18.1 %all-gather = bf16[256,1280]{1,0:T(8,128)(2,1)S(1)} all-gather(bf16[64,1280]{1,0:T(8,128)(2,1)S(1)} %dynamic-slice_select_fusion.3), channel_id=2, replica_groups=mesh['group'=1,'image'=4,'prow'=4,'pcol'=2] {'image'}, dimensions={0}, use_global_device_ids=true | all-gather | bytes 819200 | tf_op jit(solution)/shard_map/all_gather | solution.py:13
  94.6 4.2 %gather_fusion.1 = bf16[4,128,1280]{2,1,0:T(8,128)(2,1)} fusion(bf16[16,128,1280]{2,1,0:T(8,128)(2,1)} %bitcast.204, s32[1024]{0:T(1024)S(1)} %get-tuple-element.118), kind=kCustom, calls=%fused_computation.1 | custom fusion | bytes 2621456 | tf_op jit(solution)/shard_map/gather | solution.py:106
  99.8 16.3 %all-gather.1 = bf16[256,1280]{1,0:T(8,128)(2,1)S(1)} all-gather(bf16[64,1280]{1,0:T(8,128)(2,1)S(1)} %dynamic-slice_select_fusion.2), channel_id=3, replica_groups=mesh['group'=1,'image'=4,'prow'=4,'pcol'=2] {'image'}, dimensions={0}, use_global_device_ids=true | all-gather | bytes 819200 | tf_op jit(solution)/shard_map/all_gather | solution.py:13
  116.3 3.1 %gather_fusion.2 = bf16[4,128,1280]{2,1,0:T(8,128)(2,1)S(1)} fusion(bf16[16,128,1280]{2,1,0:T(8,128)(2,1)} %bitcast.205, s32[1024]{0:T(1024)S(1)} %get-tuple-element.117), kind=kCustom, calls=%fused_computation.2 | custom fusion | bytes 2621456 | tf_op jit(solution)/shard_map/gather | solution.py:106
  119.5 16.7 %all-gather.2 = bf16[256,1280]{1,0:T(8,128)(2,1)S(1)} all-gather(bf16[64,1280]{1,0:T(8,128)(2,1)S(1)} %dynamic-slice_select_fusion.1), channel_id=4, replica_groups=mesh['group'=1,'image'=4,'prow'=4,'pcol'=2] {'image'}, dimensions={0}, use_global_device_ids=true | all-gather | bytes 819200 | tf_op jit(solution)/shard_map/all_gather | solution.py:13
  136.3 3.1 %gather_fusion.3 = bf16[4,128,1280]{2,1,0:T(8,128)(2,1)S(1)} fusion(bf16[16,128,1280]{2,1,0:T(8,128)(2,1)} %bitcast.206, s32[1024]{0:T(1024)S(1)} %get-tuple-element.116), kind=kCustom, calls=%fused_computation.3 | custom fusion | bytes 2621456 | tf_op jit(solution)/shard_map/gather | solution.py:106
  139.5 15.4 %all-gather.3 = bf16[256,1280]{1,0:T(8,128)(2,1)S(1)} all-gather(bf16[64,1280]{1,0:T(8,128)(2,1)S(1)} %dynamic-slice_select_fusion), channel_id=5, replica_groups=mesh['group'=1,'image'=4,'prow'=4,'pcol'=2] {'image'}, dimensions={0}, use_global_device_ids=true | all-gather | bytes 819200 | tf_op jit(solution)/shard_map/all_gather | solution.py:13
  157.8 38.8 %all-gather.9.cloned.1.call-done = bf16[4,512,1280]{2,1,0:T(8,128)(2,1)} async-done(((bf16[4,64,1280]{2,1,0:T(8,128)(2,1)}), bf16[4,512,1280]{2,1,0:T(8,128)(2,1)}) %all-gather.9.cloned.1.call-update) | async-done | bytes 5242896 | tf_op jit(solution)/shard_map/all_gather | solution.py:109
  196.7 9.7 %pad_maximum_fusion = bf16[4096,1280]{1,0:T(8,128)(2,1)} fusion(bf16[2048,1280]{1,0:T(8,128)(2,1)} %bitcast.207, bf16[2048,1280]{1,0:T(8,128)(2,1)} %all-gather.7.cloned.1.call-done), kind=kLoop, calls=%fused_computation.23 | loop fusion | flops 20971520 | bytes 20971520 | tf_op jit(solution)/shard_map/concatenate | solution.py:112
  206.4 14.3 %copy.11 = bf16[4096,1280]{0,1:T(8,128)(2,1)} copy(bf16[4096,1280]{1,0:T(8,128)(2,1)} %pad_maximum_fusion) | data formatting | bytes 20971520 | tf_op jit(solution)/shard_map/while | solution.py:73
  220.7 48.5 %while.12 = (s32[]{:T(128)}, bf16[5,256,128]{1,2,0:T(8,128)(2,1)}, s32[5]{0:T(128)S(1)}, bf16[4096,1280]{0,1:T(8,128)(2,1)}, pred[4096]{0:T(1024)(128)(4,1)S(1)}...) while((s32[]{:T(128)}, bf16[5,256,128]{1,2,0:T(8,128)(2,1)}, ...), condition=%wide.region_9.10_spmd, body=%wide.region_6.9_spmd.sunk | while | flops 824222208 | bytes 7942902 | solution.py:73
  223.9 3.0 %fusion.91 = f32[2,256]{1,0:T(2,128)S(1)} fusion(pred[4096]{0:T(1024)(128)(4,1)S(1)} %get-tuple-element.189, bf16[256,2,64]{0,2,1:T(8,128)(2,1)S(1)} %bitcast.216, bf16[4096,2,64]{0,2,1:T(8,128)(2,1)S(1)} %bitcast.200), kind=kOutput, calls=%fused_computation.118.clone.1 | convolution fusion | flops 276828160 | bytes 1120256 | tf_op jit(solution)/shard_map/while/body/eval_jaxpr/sub | solution.py:66
  226.9 2.9 %fusion.92 = bf16[2,64,256]{2,1,0:T(8,128)(2,1)S(1)} fusion(bf16[4096,2,64]{0,2,1:T(8,128)(2,1)S(1)} %bitcast.202, f32[2,256]{1,0:T(2,128)S(1)} %fusion.91, pred[4096]{0:T(1024)(128)(4,1)S(1)} %get-tuple-element.189, bf16[256,2,64]{0,2,1:T(8,128)(2,1)S(1)} %bitcast.217, bf16[4096,2,64]{0,2,1:T(8,128)(2,1)S(1)} %bitcast.201), kind=kOutput, calls=%fused_computation.14.clone.1 | convolution fusion | flops 547394048 | bytes 2234368 | tf_op jit(solution)/shard_map/while/body/eval_jaxpr/hqk,khd->qhd/dot_general | solution.py:68
  233.6 3.0 %fusion.91 = f32[2,256]{1,0:T(2,128)S(1)} fusion(pred[4096]{0:T(1024)(128)(4,1)S(1)} %get-tuple-element.189, bf16[256,2,64]{0,2,1:T(8,128)(2,1)S(1)} %bitcast.216, bf16[4096,2,64]{0,2,1:T(8,128)(2,1)S(1)} %bitcast.200), kind=kOutput, calls=%fused_computation.118.clone.1 | convolution fusion | flops 276828160 | bytes 1120256 | tf_op jit(solution)/shard_map/while/body/eval_jaxpr/sub | solution.py:66
  236.6 2.9 %fusion.92 = bf16[2,64,256]{2,1,0:T(8,128)(2,1)S(1)} fusion(bf16[4096,2,64]{0,2,1:T(8,128)(2,1)S(1)} %bitcast.202, f32[2,256]{1,0:T(2,128)S(1)} %fusion.91, pred[4096]{0:T(1024)(128)(4,1)S(1)} %get-tuple-element.189, bf16[256,2,64]{0,2,1:T(8,128)(2,1)S(1)} %bitcast.217, bf16[4096,2,64]{0,2,1:T(8,128)(2,1)S(1)} %bitcast.201), kind=kOutput, calls=%fused_computation.14.clone.1 | convolution fusion | flops 547394048 | bytes 2234368 | tf_op jit(solution)/shard_map/while/body/eval_jaxpr/hqk,khd->qhd/dot_general | solution.py:68
  243.3 3.0 %fusion.91 = f32[2,256]{1,0:T(2,128)S(1)} fusion(pred[4096]{0:T(1024)(128)(4,1)S(1)} %get-tuple-element.189, bf16[256,2,64]{0,2,1:T(8,128)(2,1)S(1)} %bitcast.216, bf16[4096,2,64]{0,2,1:T(8,128)(2,1)S(1)} %bitcast.200), kind=kOutput, calls=%fused_computation.118.clone.1 | convolution fusion | flops 276828160 | bytes 1120256 | tf_op jit(solution)/shard_map/while/body/eval_jaxpr/sub | solution.py:66
  246.3 2.9 %fusion.92 = bf16[2,64,256]{2,1,0:T(8,128)(2,1)S(1)} fusion(bf16[4096,2,64]{0,2,1:T(8,128)(2,1)S(1)} %bitcast.202, f32[2,256]{1,0:T(2,128)S(1)} %fusion.91, pred[4096]{0:T(1024)(128)(4,1)S(1)} %get-tuple-element.189, bf16[256,2,64]{0,2,1:T(8,128)(2,1)S(1)} %bitcast.217, bf16[4096,2,64]{0,2,1:T(8,128)(2,1)S(1)} %bitcast.201), kind=kOutput, calls=%fused_computation.14.clone.1 | convolution fusion | flops 547394048 | bytes 2234368 | tf_op jit(solution)/shard_map/while/body/eval_jaxpr/hqk,khd->qhd/dot_general | solution.py:68
  253.0 3.0 %fusion.91 = f32[2,256]{1,0:T(2,128)S(1)} fusion(pred[4096]{0:T(1024)(128)(4,1)S(1)} %get-tuple-element.189, bf16[256,2,64]{0,2,1:T(8,128)(2,1)S(1)} %bitcast.216, bf16[4096,2,64]{0,2,1:T(8,128)(2,1)S(1)} %bitcast.200), kind=kOutput, calls=%fused_computation.118.clone.1 | convolution fusion | flops 276828160 | bytes 1120256 | tf_op jit(solution)/shard_map/while/body/eval_jaxpr/sub | solution.py:66
  256.0 2.9 %fusion.92 = bf16[2,64,256]{2,1,0:T(8,128)(2,1)S(1)} fusion(bf16[4096,2,64]{0,2,1:T(8,128)(2,1)S(1)} %bitcast.202, f32[2,256]{1,0:T(2,128)S(1)} %fusion.91, pred[4096]{0:T(1024)(128)(4,1)S(1)} %get-tuple-element.189, bf16[256,2,64]{0,2,1:T(8,128)(2,1)S(1)} %bitcast.217, bf16[4096,2,64]{0,2,1:T(8,128)(2,1)S(1)} %bitcast.201), kind=kOutput, calls=%fused_computation.14.clone.1 | convolution fusion | flops 547394048 | bytes 2234368 | tf_op jit(solution)/shard_map/while/body/eval_jaxpr/hqk,khd->qhd/dot_general | solution.py:68
  262.7 3.0 %fusion.91 = f32[2,256]{1,0:T(2,128)S(1)} fusion(pred[4096]{0:T(1024)(128)(4,1)S(1)} %get-tuple-element.189, bf16[256,2,64]{0,2,1:T(8,128)(2,1)S(1)} %bitcast.216, bf16[4096,2,64]{0,2,1:T(8,128)(2,1)S(1)} %bitcast.200), kind=kOutput, calls=%fused_computation.118.clone.1 | convolution fusion | flops 276828160 | bytes 1120256 | tf_op jit(solution)/shard_map/while/body/eval_jaxpr/sub | solution.py:66
  265.7 2.9 %fusion.92 = bf16[2,64,256]{2,1,0:T(8,128)(2,1)S(1)} fusion(bf16[4096,2,64]{0,2,1:T(8,128)(2,1)S(1)} %bitcast.202, f32[2,256]{1,0:T(2,128)S(1)} %fusion.91, pred[4096]{0:T(1024)(128)(4,1)S(1)} %get-tuple-element.189, bf16[256,2,64]{0,2,1:T(8,128)(2,1)S(1)} %bitcast.217, bf16[4096,2,64]{0,2,1:T(8,128)(2,1)S(1)} %bitcast.201), kind=kOutput, calls=%fused_computation.14.clone.1 | convolution fusion | flops 547394048 | bytes 2234368 | tf_op jit(solution)/shard_map/while/body/eval_jaxpr/hqk,khd->qhd/dot_general | solution.py:68
  (95 shorter events, 40.5 us)
Async XLA Ops:
  7.2 21.2 %copy-start = (bf16[640,640]{1,0:T(8,128)(2,1)S(1)}, bf16[640,640]{1,0:T(8,128)(2,1)}, u32[]{:S(2)}) copy-start(bf16[640,640]{1,0:T(8,128)(2,1)} %param.15) | copy-start | bytes 2457604
  7.2 66.2 %all-gather.7.cloned.1.call-start = ((), (), s32[]{:S(2)}) async-start(), calls=%async_computation | async-start | bytes 5898240 | tf_op jit(solution)/shard_map/all_gather | solution.py:99
  7.2 16.8 %copy-start.3 = (bf16[3,3,640,640]{3,2,1,0:T(8,128)(2,1)S(1)}, bf16[3,3,640,640]{3,2,1,0:T(8,128)(2,1)}, u32[]{:S(2)}) copy-start(bf16[3,3,640,640]{3,2,1,0:T(8,128)(2,1)} %param.12) | copy-start | bytes 22118404
  8.6 8.2 %collective-permute-start = (bf16[1,1,32,640]{3,2,1,0:T(8,128)(2,1)S(1)}, bf16[1,1,32,640]{3,2,1,0:T(8,128)(2,1)S(1)}, u32[]{:S(2)}, u32[]{:S(2)}) collective-permute-start(bf16[1,1,32,640]{3,2,1,0:T(8,128)(2,1)S(1)} %get-tuple-element.104), channel_id=1, source_target_pairs={{0,2},{2,4},{4,6},{1,3},{3,5},{5,7},{8,10},{10,12},{12,14},{9,11},... | collective-permute-start | bytes 122888 | tf_op jit(solution)/shard_map/ppermute | solution.py:26
  13.7 5.9 %collective-permute-start.1 = (bf16[1,1,32,640]{3,2,1,0:T(8,128)(2,1)S(1)}, bf16[1,1,32,640]{3,2,1,0:T(8,128)(2,1)S(1)}, u32[]{:S(2)}, u32[]{:S(2)}) collective-permute-start(bf16[1,1,32,640]{3,2,1,0:T(8,128)(2,1)S(1)} %get-tuple-element.105), channel_id=1, source_target_pairs={{2,0},{4,2},{6,4},{3,1},{5,3},{7,5},{10,8},{12,10},{14,12},{11,9},... | collective-permute-start | bytes 122888 | tf_op jit(solution)/shard_map/ppermute | solution.py:28
  19.7 4.8 %collective-permute-start.2 = (bf16[1,10,1,640]{3,2,1,0:T(2,128)(2,1)S(1)}, bf16[1,10,1,640]{3,2,1,0:T(2,128)(2,1)S(1)}, u32[]{:S(2)}, u32[]{:S(2)}) collective-permute-start(bf16[1,10,1,640]{3,2,1,0:T(2,128)(2,1)S(1)} %get-tuple-element.102), channel_id=1, source_target_pairs={{0,1},{2,3},{4,5},{6,7},{8,9},{10,11},{12,13},{14,15},{16,17},{18,... | collective-permute-start | bytes 38408 | tf_op jit(solution)/shard_map/ppermute | solution.py:26
  21.0 6.1 %copy-start.2 = (bf16[1,8,32,640]{3,2,1,0:T(8,128)(2,1)S(1)}, bf16[1,8,32,640]{3,2,1,0:T(8,128)(2,1)}, u32[]{:S(2)}) copy-start(bf16[1,8,32,640]{3,2,1,0:T(8,128)(2,1)} %param.11) | copy-start | bytes 983044
  21.0 3.5 %collective-permute-start.3 = (bf16[1,10,1,640]{3,2,1,0:T(2,128)(2,1)S(1)}, bf16[1,10,1,640]{3,2,1,0:T(2,128)(2,1)S(1)}, u32[]{:S(2)}, u32[]{:S(2)}) collective-permute-start(bf16[1,10,1,640]{3,2,1,0:T(2,128)(2,1)S(1)} %get-tuple-element.103), channel_id=1, source_target_pairs={{1,0},{3,2},{5,4},{7,6},{9,8},{11,10},{13,12},{15,14},{17,16},{19,... | collective-permute-start | bytes 38408 | tf_op jit(solution)/shard_map/ppermute | solution.py:28
  25.6 3.2 %copy-start.4 = (bf16[640,640]{1,0:T(8,128)(2,1)S(1)}, bf16[640,640]{1,0:T(8,128)(2,1)}, u32[]{:S(2)}) copy-start(bf16[640,640]{1,0:T(8,128)(2,1)} %param.14) | copy-start | bytes 2457604
  26.6 3.7 %copy-start.5 = (s32[4]{0:T(128)S(1)}, s32[4]{0:T(128)}, u32[]{:S(2)}) copy-start(s32[4]{0:T(128)} %param.17) | copy-start | bytes 52
  26.6 6.9 %copy-start.6 = (s32[4,16]{1,0:T(4,128)S(1)}, s32[4,16]{1,0:T(4,128)}, u32[]{:S(2)}) copy-start(s32[4,16]{1,0:T(4,128)} %param.18) | copy-start | bytes 772
  27.8 88.5 %copy-start.1 = (bf16[1,8,32,640]{3,2,1,0:T(8,128)(2,1)}, bf16[1,8,32,640]{3,2,1,0:T(8,128)(2,1)S(1)}, u32[]{:S(2)}) copy-start(bf16[1,8,32,640]{3,2,1,0:T(8,128)(2,1)S(1)} %get-tuple-element.115) | copy-start | bytes 983044
  30.2 166.4 %all-gather.9.cloned.1.call-start = ((), (), s32[]{:S(2)}) async-start(), calls=%async_computation.1 | async-start | bytes 5898240 | tf_op jit(solution)/shard_map/all_gather | solution.py:109
  98.8 57.1 %copy-start.7 = (s32[4]{0:T(128)S(1)}, s32[4]{0:T(128)}, u32[]{:S(2)}) copy-start(s32[4]{0:T(128)} %param.19) | copy-start | bytes 52
Sparse Core Ops, SparseCore 0:
  30.4 42.9 all-gather.6
  156.1 40.5 all-gather.8
